TPU v7x, 32 devices: a whole 2x2x4 slice. The times are simulated.
32 devices in a mesh: dp: 2 (over x), ts: 16 (over z, y, core).
Axes of the slice: x: 2, y: 2, z: 4, core: 2. Of those that a mesh axis runs over, the one named last changes fastest.
Arguments:
- clip_video: bfloat16 [64, 4, 40, 128], P(('dp', 'ts')), may hold values from -6 to 6
- conv_weight: bfloat16 [3, 3, 3, 128, 128], replicated, may hold values from -0.109375 to 0.109375
- embed_weight: bfloat16 [128, 5120], replicated, may hold values from -0.5 to 0.5
- gain_spatial: float32 [5120], replicated, may hold values from 0.5 to 1.5
- gain_temporal: float32 [5120], replicated, may hold values from 0.5 to 1.5
- input_spatial: bfloat16 [5120, 384], P(('dp', 'ts')), may hold values from -0.078125 to 0.078125
- input_temporal: bfloat16 [5120, 384], P(('dp', 'ts')), may hold values from -0.078125 to 0.078125
- output_spatial: bfloat16 [128, 5120], replicated, may hold values from -2 to 2
- output_temporal: bfloat16 [128, 5120], replicated, may hold values from -2 to 2
- cotangent: bfloat16 [64, 4, 40, 5120], P(('dp', 'ts')), may hold values from -6 to 6
Outputs:
- layer_output: bfloat16 [64, 4, 40, 5120], P(('dp', 'ts'))
- grad_spatial: float32 [5120, 384], P(('dp', 'ts'))
All inputs are finite; a program needn't handle non-finite values.
Results may differ from a plain program's by a relative error of at most 0.015.
Values may be sent and summed in bfloat16 or wider, within the bound.
A program may use at most 128 MiB of HBM per device.

v0:
```python
import jax
import jax.numpy as jnp
from jax import lax
from jax.sharding import PartitionSpec as P

FR = 16
epsilon = 1e-06
masked = -1e30
F32 = jnp.float32
BF16 = jnp.bfloat16


def mm(a, b, dims=((1,), (0,))):
    return lax.dot_general(a, b, (dims, ((), ())), preferred_element_type=F32)


def mm_t(a, b):
    return mm(a, b, ((1,), (1,)))


def t_mm(a, b):
    return mm(a, b, ((0,), (0,)))


def wide_mm(a, b):
    high = b.astype(BF16)
    low = (b - high.astype(F32)).astype(BF16)
    return mm(a, high) + mm(a, low)


def conv_local(volume, weight, count):
    frames, height, columns, channels = volume.shape
    padded = jnp.pad(volume, ((0, 0), (1, 1), (1, 1), (0, 0)))
    summed = jnp.zeros((count * height * columns, weight.shape[-1]), F32)
    for a in range(3):
        for b in range(3):
            for e in range(3):
                window = padded[2 - a : 2 - a + count, b : b + height, e : e + columns, :]
                summed = summed + mm(window.reshape(-1, channels), weight[a, b, e])
    return summed


def attend_forward(q, k, v, allowed):
    scores = mm_t(q, k) * q.shape[-1] ** (-0.5)
    scores = jnp.where(allowed, scores, masked)
    raised = jnp.exp(scores - jnp.max(scores, axis=-1, keepdims=True))
    attend = raised / jnp.sum(raised, axis=-1, keepdims=True)
    return (mm(attend.astype(BF16), v).astype(BF16), attend)


def attend_backward(q, k, v, attend, g):
    scale = q.shape[-1] ** (-0.5)
    grad_attend = mm_t(g, v)
    grad_values = t_mm(attend.astype(BF16), g)
    inner = jnp.sum(grad_attend * attend, axis=-1, keepdims=True)
    grad_scores = (attend * (grad_attend - inner)).astype(BF16)
    grad_q = mm(grad_scores, k) * scale
    grad_k = t_mm(grad_scores, q) * scale
    return jnp.concatenate([grad_q, grad_k, grad_values], axis=-1).astype(BF16)


def shards(
    clip_video,
    conv_weight,
    embed_weight,
    gain_spatial,
    gain_temporal,
    input_spatial,
    input_temporal,
    output_spatial,
    output_temporal,
    cotangent,
):
    frames, height, columns, channels = clip_video.shape
    rows, triple = input_spatial.shape
    head = triple // 3
    width = embed_weight.shape[-1]
    places = height * columns
    tokens = frames * places
    ts = lax.axis_size("ts")
    team = FR // frames
    share = places // team
    groups = [[c * team + i for i in range(team)] for c in range(ts // team)]
    me = lax.axis_index("dp") * ts + lax.axis_index("ts")
    route = [(i - 1, i) for i in range(1, ts)]
    prior = lax.ppermute(clip_video, "ts", route)
    volume = jnp.concatenate([prior, clip_video], axis=0)
    basis = jnp.concatenate([embed_weight, output_spatial], axis=0)
    window = lax.dynamic_slice(basis, (0, me * rows), (basis.shape[0], rows)).astype(F32)
    gain_s = lax.dynamic_slice(gain_spatial, (me * rows,), (rows,))
    gain_t = lax.dynamic_slice(gain_temporal, (me * rows,), (rows,))
    embed_rows = (window[:channels] * gain_s).astype(BF16)
    part = jnp.concatenate(
        [mm(embed_rows, input_spatial), mm((window * gain_t).astype(BF16), input_temporal)], axis=0
    )
    mixed = lax.psum(part.astype(BF16), ("dp", "ts"))
    map_space, map_time = (mixed[:channels], mixed[channels:])
    gram = mm_t(basis, basis)
    cotangent_rows = cotangent.reshape(tokens, width)
    grad_mix_time = mm_t(cotangent_rows, output_temporal).astype(BF16)
    grad_direct = mm_t(cotangent_rows, output_spatial)
    features = jax.nn.gelu(conv_local(volume, conv_weight, frames), approximate=True).astype(BF16)
    squares = jnp.sum(
        wide_mm(features, gram[:channels, :channels]) * features.astype(F32), axis=-1, keepdims=True
    )
    factor_one = lax.rsqrt(jnp.maximum(squares, 0.0) / width + epsilon)
    packed_one = (mm(features, map_space) * factor_one).astype(BF16)
    place = jnp.arange(tokens)
    same_frame = place[:, None] // places == place[None, :] // places
    q, k, v = (packed_one[:, :head], packed_one[:, head : 2 * head], packed_one[:, 2 * head :])
    mixture_one, attend_one = attend_forward(q, k, v, same_frame)
    joint = jnp.concatenate([features, mixture_one], axis=-1)
    spread = wide_mm(joint, gram)
    squares = jnp.sum(spread * joint.astype(F32), axis=-1, keepdims=True)
    factor_two = lax.rsqrt(jnp.maximum(squares, 0.0) / width + epsilon)
    packed_two = (mm(joint, map_time) * factor_two).astype(BF16)
    sent = jnp.concatenate([packed_two, grad_mix_time], axis=-1).reshape(frames, places, 4 * head)
    got = lax.all_to_all(
        sent, "ts", split_axis=1, concat_axis=0, tiled=True, axis_index_groups=groups
    ).reshape(FR * share, 4 * head)
    spot = jnp.arange(FR * share)
    allowed = (spot[:, None] % share == spot[None, :] % share) & (spot[:, None] >= spot[None, :])
    tq, tk, tv, tg = (got[:, i * head : (i + 1) * head] for i in range(4))
    mixture_two, attend_two = attend_forward(tq, tk, tv, allowed)
    grad_two = attend_backward(tq, tk, tv, attend_two, tg)
    back = jnp.concatenate([mixture_two, grad_two], axis=-1).reshape(FR, share, 4 * head)
    home = lax.all_to_all(
        back, "ts", split_axis=0, concat_axis=1, tiled=True, axis_index_groups=groups
    ).reshape(tokens, 4 * head)
    mixture_two, grad_two = (home[:, :head], home[:, head:])
    output = mm(
        jnp.concatenate([joint, mixture_two], axis=-1),
        jnp.concatenate([basis, output_temporal], axis=0),
    ).astype(BF16)
    inner = jnp.sum(grad_two.astype(F32) * packed_two.astype(F32), axis=-1, keepdims=True)
    grad_mix_one = (
        grad_direct
        + factor_two * mm_t(grad_two, map_time[channels:])
        - factor_two**2 * inner / width * spread[:, channels:]
    ).astype(BF16)
    grad_one = attend_backward(q, k, v, attend_one, grad_mix_one)
    scaled = (features.astype(F32) * factor_one).astype(BF16)
    core = lax.psum(t_mm(scaled, grad_one).astype(BF16), ("dp", "ts"))
    return (output.reshape(frames, height, columns, width), t_mm(embed_rows, core))


def solution(mesh):
    placed = (
        P(("dp", "ts"), None, None, None),
        P(),
        P(),
        P(),
        P(),
        P(("dp", "ts"), None),
        P(("dp", "ts"), None),
        P(),
        P(),
        P(("dp", "ts"), None, None, None),
    )
    return jax.shard_map(
        shards,
        mesh=mesh,
        in_specs=placed,
        out_specs=(P(("dp", "ts"), None, None, None), P(("dp", "ts"), None)),
        check_vma=False,
    )
```

profile of v0, /device:TPU:8, one launch (start us, length us, event | category | flops | bytes accessed | tf_op | source)
XLA Modules:
  0.0 330.4 jit_solution(1640951019662262618)
XLA Ops:
  7.2 2.2 collective-permute-start
  9.4 2.5 constant_dynamic-update-slice_fusion.3
  11.9 2.5 constant_dynamic-update-slice_fusion.2
  14.4 1.0 dynamic-slice_convert_fusion
  15.4 0.8 dynamic_slice.10
  16.3 0.8 dynamic_slice.11
  17.0 1.2 convolution_convert_fusion.1
  18.2 1.1 convolution_convert_fusion.3
  19.3 0.7 pad_maximum_fusion.2
  20.1 3.5 %fusion.148 = f32[256,256]{1,0:T(8,128)S(1)} fusion(bf16[256,5120]{1,0:T(8,128)(2,1)} %constant_dynamic-update-slice_fusion.2), kind=kOutput, calls=%fused_computation.247 | convolution fusion | flops 671088640 | bytes 2883584 | tf_op jit(solution)/shard_map/dot_general | solution.py:14
  23.7 1.0 convolution_convert_fusion.4
  24.8 0.2 pad_slice_fusion
  25.1 0.8 copy-done.8
  26.2 0.2 convolution_add_fusion.27
  26.7 0.2 convolution_add_fusion.24
  27.1 0.2 convolution_add_fusion.21
  27.3 0.2 convolution_add_fusion.20
  27.5 0.2 convolution_add_fusion.19
  27.6 0.2 convolution_add_fusion.18
  27.9 0.2 convolution_add_fusion.16
  28.4 0.2 convolution_add_fusion.13
  28.6 0.2 convolution_add_fusion.12
  28.7 0.2 convolution_add_fusion.11
  28.9 0.2 convolution_add_fusion.10
  29.6 0.2 fusion.11
  30.0 0.2 fusion.43
  30.4 0.3 fusion.17
  30.7 120.0 %all-reduce.4.cloned.1.call-done = bf16[384,384]{1,0:T(8,128)(2,1)} async-done(((bf16[384,384]{1,0:T(8,128)(2,1)}), bf16[384,384]{1,0:T(8,128)(2,1)}) %all-reduce.4.cloned.1.call-update) | async-done | bytes 294928 | tf_op jit(solution)/shard_map/psum | solution.py:96
  150.8 1.1 fusion.7
  151.9 0.2 fusion.146
  152.3 0.7 copy-done.1
  153.0 0.3 convolution_convert_fusion.8
  153.3 0.2 fusion.71
  153.5 0.9 multiply_reduce_fusion.3
  154.4 0.3 fusion.8
  154.7 0.7 copy-done.7
  155.4 1.0 copy.12
  156.5 4.2 %all-to-all-start = ((bf16[2,160,512]{2,0,1:T(2,128)(2,1)}), bf16[2,160,512]{2,0,1:T(2,128)(2,1)}, u32[]{:S(2)}, u32[]{:S(2)}) async-start(bf16[2,160,512]{2,0,1:T(2,128)(2,1)} %copy.12), calls=%async_computation | async-start | bytes 655360 | tf_op jit(solution)/shard_map/all_to_all | solution.py:118
  160.7 6.2 %all-to-all-done = bf16[2,160,512]{2,0,1:T(2,128)(2,1)} async-done(((bf16[2,160,512]{2,0,1:T(2,128)(2,1)}), bf16[2,160,512]{2,0,1:T(2,128)(2,1)}, u32[]{:S(2)}, u32[]{:S(2)}) %all-to-all-start) | async-done | bytes 327712 | tf_op jit(solution)/shard_map/all_to_all | solution.py:118
  166.9 1.8 copy.13
  168.7 1.8 reshape.248
  170.5 1.2 fusion.147
  171.8 1.2 convolution_convert_fusion.7
  173.0 0.2 multiply_reduce_fusion.2
  173.4 0.3 fusion.12
  173.7 0.2 fusion.13
  173.9 0.2 convolution_convert_fusion.6
  174.1 0.8 pad_maximum_fusion.1
  174.9 1.8 reshape.249
  176.7 10.8 %all_to_all.30 = bf16[16,20,512]{2,1,0:T(8,128)(2,1)S(1)} all-to-all(bf16[16,20,512]{2,1,0:T(8,128)(2,1)} %reshape.249), channel_id=1, replica_groups={{0,1,2,3,4,5,6,7},{8,9,10,11,12,13,14,15},{16,17,18,19,20,21,22,23},{24..., dimensions={0} | all-to-all | bytes 655360 | tf_op jit(solution)/shard_map/all_to_all | solution.py:127
  187.5 0.3 copy.18
  187.8 0.9 copy.15
  188.7 1.8 reshape.250
  190.5 1.2 multiply_reduce_fusion.1
  191.7 1.3 convolution_multiply_fusion.6
  193.0 2.4 fusion.16
  195.5 0.3 multiply_reduce_fusion
  195.9 0.3 fusion.14
  196.2 0.2 fusion.15
  196.4 0.2 convolution_convert_fusion.5
  196.6 1.0 convolution_convert_fusion.2
  197.7 5.7 %convolution_convert_fusion = bf16[320,5120]{1,0:T(8,128)(2,1)} fusion(bf16[128,5120]{1,0:T(8,128)(2,1)} %param.18, bf16[128,5120]{1,0:T(8,128)(2,1)} %param.17, bf16[128,5120]{1,0:T(8,128)(2,1)} %param.12, bf16[320,128]{1,0:T(8,128)(2,1)S(1)} %slice-done, bf16[320,128]{1,0:T(8,128)(2,1)S(1)} %convolution_convert_fusion.8, bf16[320,128]{1,0:T(8,128)(2,1)S(1)} %fusion.43), kind=kOutput, calls=%fused_computation | convolution fusion | flops 1272463360 | bytes 7454720 | tf_op jit(solution)/shard_map/dot_general | solution.py:14
  203.3 118.4 %all-reduce.6.cloned.1.call-done = bf16[128,384]{1,0:T(8,128)(2,1)} async-done(((bf16[128,384]{1,0:T(8,128)(2,1)}), bf16[128,384]{1,0:T(8,128)(2,1)}) %all-reduce.6.cloned.1.call-update) | async-done | bytes 98320 | tf_op jit(solution)/shard_map/psum | solution.py:143
  321.7 1.9 fusion.129
  (62 shorter events, 3.2 us)
Async XLA Ops:
  7.2 16.5 %copy-start = (bf16[2,4,40,5120]{3,2,1,0:T(8,128)(2,1)S(1)}, bf16[2,4,40,5120]{3,2,1,0:T(8,128)(2,1)}, u32[]{:S(2)}) copy-start(bf16[2,4,40,5120]{3,2,1,0:T(8,128)(2,1)} %param.19) | copy-start | bytes 9830404
  7.2 143.6 %all-reduce.4.cloned.1.call-start = ((), (), s32[]{:S(2)}) async-start(), calls=%async_computation.2 | async-start | bytes 589824 | tf_op jit(solution)/shard_map/psum | solution.py:96
  7.2 17.5 %collective-permute-start = (bf16[2,4,40,128]{3,2,1,0:T(8,128)(2,1)}, bf16[2,4,40,128]{3,2,1,0:T(8,128)(2,1)S(1)}, u32[]{:S(2)}, u32[]{:S(2)}) collective-permute-start(bf16[2,4,40,128]{3,2,1,0:T(8,128)(2,1)} %param.10), channel_id=1, source_target_pairs={{0,1},{1,2},{2,3},{3,4},{4,5},{5,6},{6,7},{7,8},{8,9},{9,10},{10,1... | collective-permute-start | bytes 245768 | tf_op jit(solution)/shard_map/ppermute | solution.py:86
  9.4 7.6 %copy-start.13 = (bf16[160,384]{1,0:T(8,128)(2,1)S(1)}, bf16[160,384]{1,0:T(8,128)(2,1)}, u32[]{:S(2)}) copy-start(bf16[160,384]{1,0:T(8,128)(2,1)} %param.16) | copy-start | bytes 368644
  15.4 2.8 copy-start.6
  20.1 3.6 %copy-start.5 = (bf16[128,5120]{1,0:T(8,128)(2,1)S(1)}, bf16[128,5120]{1,0:T(8,128)(2,1)}, u32[]{:S(2)}) copy-start(bf16[128,5120]{1,0:T(8,128)(2,1)} %param.18) | copy-start | bytes 3932164
  23.6 6.8 %copy-start.3 = (f32[256,256]{1,0:T(8,128)}, f32[256,256]{1,0:T(8,128)S(1)}, u32[]{:S(2)}) copy-start(f32[256,256]{1,0:T(8,128)S(1)} %fusion.148) | copy-start | bytes 786436
  23.7 1.1 copy-start.12
  24.7 1.2 copy-start.8
  150.7 2.5 copy-start.4
  151.9 1.3 copy-start.10
  151.9 2.5 copy-start.14
  152.2 0.8 copy-start.1
  154.7 0.7 copy-start.7
  156.5 10.4 %all-to-all-start = ((bf16[2,160,512]{2,0,1:T(2,128)(2,1)}), bf16[2,160,512]{2,0,1:T(2,128)(2,1)}, u32[]{:S(2)}, u32[]{:S(2)}) async-start(bf16[2,160,512]{2,0,1:T(2,128)(2,1)} %copy.12), calls=%async_computation | async-start | bytes 655360 | tf_op jit(solution)/shard_map/all_to_all | solution.py:118
  160.7 161.0 %all-reduce.6.cloned.1.call-start = ((), (), s32[]{:S(2)}) async-start(), calls=%async_computation.3 | async-start | bytes 196608 | tf_op jit(solution)/shard_map/psum | solution.py:143
  170.5 2.5 copy-start.9
  193.0 2.4 copy-start.2
  193.0 2.4 copy-start.11
  195.7 1.9 slice-start
Sparse Core Ops, SparseCore 0:
  20.2 130.4 all-reduce.3
  197.8 123.8 all-reduce.5
where the time goes:
time: 331 us; the launch traced here: 330 us
  waiting for transfers between devices  245 us (74%)
  matrix products  31.3 us (9%)
  local copies, waits for them, and re-layouts  18.4 us (6%)
  between operations  14.5 us (4%)
  blocking collectives  10.8 us (3%)
  starting transfers between devices  6.42 us (2%)
  other arithmetic  4.29 us (1%)
    psum x1, waiting for transfers between devices, shards(): mixed = lax.psum(part.astype(BF16), ('dp', 'ts'))  120 us
    psum x1, waiting for transfers between devices, shards(): core = lax.psum(t_mm(scaled, grad_one).astype(BF16), ('dp', 'ts'))  118 us
    dot_general x54, matrix products, mm(): return lax.dot_general(a, b, (dims, ((), ())), preferred_element_type=F32)  31.3 us
    all_to_all x1, blocking collectives, shards(): lax.all_to_all(back, 'ts', split_axis=0, concat_axis=1, tiled=True, axis_...  10.8 us
  transfers between devices with their start and end apart: 4, of which 3 were waited for; matrix products, arithmetic and copies ran while one was open for 8% of the time, Pallas kernels for 0%

commit v1 on v0

--- a/solution.py
+++ b/solution.py
@@ -93,7 +93,8 @@
     part = jnp.concatenate(
         [mm(embed_rows, input_spatial), mm((window * gain_t).astype(BF16), input_temporal)], axis=0
     )
-    mixed = lax.psum(part.astype(BF16), ("dp", "ts"))
+    xx = part.astype(BF16)
+    mixed = lax.psum(lax.psum(xx, "ts"), "dp")
     map_space, map_time = (mixed[:channels], mixed[channels:])
     gram = mm_t(basis, basis)
     cotangent_rows = cotangent.reshape(tokens, width)

time: 331 us -> 318 us (0.961)
  waiting for transfers between devices: 245 us -> 230 us
    psum x1 -> x2, waiting for transfers between devices: 120 us -> 106 us  [shards(): mixed = lax.psum(lax.psum(xx, 'ts'), 'dp')]
  transfers between devices with their start and end apart: 4 -> 5, of which waited for: 3 -> 4; matrix products, arithmetic and copies ran while one was open for 8% -> 9% of each run, Pallas kernels for 0% -> 0%
where the time goes in v1:
time: 318 us; the launch traced here: 317 us
  waiting for transfers between devices  230 us (72%)
  matrix products  32.7 us (10%)
  local copies, waits for them, and re-layouts  18.5 us (6%)
  between operations  14.2 us (4%)
  blocking collectives  10.8 us (3%)
  starting transfers between devices  6.78 us (2%)
  other arithmetic  4.29 us (1%)
    psum x1, waiting for transfers between devices, shards(): core = lax.psum(t_mm(scaled, grad_one).astype(BF16), ('dp', 'ts'))  118 us
    psum x2, waiting for transfers between devices, shards(): mixed = lax.psum(lax.psum(xx, 'ts'), 'dp')  106 us
    dot_general x54, matrix products, mm(): return lax.dot_general(a, b, (dims, ((), ())), preferred_element_type=F32)  32.7 us
    all_to_all x1, blocking collectives, shards(): lax.all_to_all(back, 'ts', split_axis=0, concat_axis=1, tiled=True, axis_...  10.8 us
  transfers between devices with their start and end apart: 5, of which 4 were waited for; matrix products, arithmetic and copies ran while one was open for 9% of the time, Pallas kernels for 0%

profile of v1, /device:TPU:8, one launch (start us, length us, event | category | flops | bytes accessed | tf_op | source)
XLA Modules:
  0.0 317.3 jit_solution(11479207326354246197)
XLA Ops:
  7.2 2.2 collective-permute-start
  9.4 2.5 constant_dynamic-update-slice_fusion.3
  11.9 2.5 constant_dynamic-update-slice_fusion.2
  14.4 1.0 dynamic-slice_convert_fusion
  15.4 0.8 dynamic_slice.10
  16.3 0.8 dynamic_slice.11
  17.0 1.2 convolution_convert_fusion.1
  18.2 1.1 convolution_convert_fusion.3
  19.3 0.7 pad_maximum_fusion.2
  20.2 3.5 %fusion.148 = f32[256,256]{1,0:T(8,128)S(1)} fusion(bf16[256,5120]{1,0:T(8,128)(2,1)} %constant_dynamic-update-slice_fusion.2), kind=kOutput, calls=%fused_computation.247 | convolution fusion | flops 671088640 | bytes 2883584 | tf_op jit(solution)/shard_map/dot_general | solution.py:14
  23.7 1.6 convolution_convert_fusion.4
  25.4 0.2 pad_slice_fusion
  25.7 0.8 copy-done.8
  26.7 0.2 fusion.76
  26.8 0.2 convolution_add_fusion.27
  27.2 0.2 convolution_add_fusion.25
  27.5 0.2 convolution_add_fusion.23
  27.6 0.2 convolution_add_fusion.22
  28.4 0.2 convolution_add_fusion.17
  28.8 0.2 convolution_add_fusion.15
  28.9 0.2 convolution_add_fusion.14
  29.7 0.2 convolution_add_fusion.9
  30.1 0.2 convolution_add_fusion.7
  30.2 0.2 fusion.11
  30.7 0.2 fusion.43
  31.1 81.8 %all-reduce.5.cloned.1.call-done = bf16[384,384]{1,0:T(8,128)(2,1)} async-done(((bf16[384,384]{1,0:T(8,128)(2,1)}), bf16[384,384]{1,0:T(8,128)(2,1)}) %all-reduce.5.cloned.1.call-update) | async-done | bytes 294928 | tf_op jit(solution)/shard_map/psum | solution.py:97
  112.9 1.1 fusion.17
  114.0 23.9 %all-reduce.7.cloned.1.call-done = bf16[384,384]{1,0:T(8,128)(2,1)} async-done(((bf16[384,384]{1,0:T(8,128)(2,1)}), bf16[384,384]{1,0:T(8,128)(2,1)}) %all-reduce.7.cloned.1.call-update) | async-done | bytes 294928 | tf_op jit(solution)/shard_map/psum | solution.py:97
  138.0 1.1 fusion.7
  139.1 0.2 fusion.146
  139.5 0.6 copy-done.1
  140.2 0.3 convolution_convert_fusion.8
  140.5 0.2 fusion.71
  140.7 0.9 multiply_reduce_fusion.3
  141.6 0.3 fusion.8
  141.9 0.7 copy-done.7
  142.6 1.1 copy.12
  143.7 4.5 %all-to-all-start = ((bf16[2,160,512]{2,0,1:T(2,128)(2,1)}), bf16[2,160,512]{2,0,1:T(2,128)(2,1)}, u32[]{:S(2)}, u32[]{:S(2)}) async-start(bf16[2,160,512]{2,0,1:T(2,128)(2,1)} %copy.12), calls=%async_computation | async-start | bytes 655360 | tf_op jit(solution)/shard_map/all_to_all | solution.py:119
  148.2 6.3 %all-to-all-done = bf16[2,160,512]{2,0,1:T(2,128)(2,1)} async-done(((bf16[2,160,512]{2,0,1:T(2,128)(2,1)}), bf16[2,160,512]{2,0,1:T(2,128)(2,1)}, u32[]{:S(2)}, u32[]{:S(2)}) %all-to-all-start) | async-done | bytes 327712 | tf_op jit(solution)/shard_map/all_to_all | solution.py:119
  154.5 1.8 copy.13
  156.2 1.8 reshape.248
  158.0 1.2 fusion.147
  159.4 1.2 convolution_convert_fusion.7
  160.6 0.3 multiply_reduce_fusion.2
  160.9 0.3 fusion.12
  161.2 0.2 fusion.13
  161.5 0.2 convolution_convert_fusion.6
  161.7 0.8 pad_maximum_fusion.1
  162.5 1.8 reshape.249
  164.2 10.8 %all_to_all.30 = bf16[16,20,512]{2,1,0:T(8,128)(2,1)S(1)} all-to-all(bf16[16,20,512]{2,1,0:T(8,128)(2,1)} %reshape.249), channel_id=1, replica_groups={{0,1,2,3,4,5,6,7},{8,9,10,11,12,13,14,15},{16,17,18,19,20,21,22,23},{24..., dimensions={0} | all-to-all | bytes 655360 | tf_op jit(solution)/shard_map/all_to_all | solution.py:128
  175.0 0.3 copy.18
  175.3 0.9 copy.15
  176.3 1.8 reshape.250
  178.1 1.2 multiply_reduce_fusion.1
  179.3 1.3 convolution_multiply_fusion.6
  180.6 2.4 fusion.16
  183.0 0.2 multiply_reduce_fusion
  183.4 0.3 fusion.14
  183.7 0.2 fusion.15
  183.9 0.2 convolution_convert_fusion.5
  184.2 1.0 convolution_convert_fusion.2
  185.2 5.7 %convolution_convert_fusion = bf16[320,5120]{1,0:T(8,128)(2,1)} fusion(bf16[128,5120]{1,0:T(8,128)(2,1)} %param.18, bf16[128,5120]{1,0:T(8,128)(2,1)} %param.17, bf16[128,5120]{1,0:T(8,128)(2,1)} %param.12, bf16[320,128]{1,0:T(8,128)(2,1)S(1)} %slice-done, bf16[320,128]{1,0:T(8,128)(2,1)S(1)} %convolution_convert_fusion.8, bf16[320,128]{1,0:T(8,128)(2,1)S(1)} %fusion.43), kind=kOutput, calls=%fused_computation | convolution fusion | flops 1272463360 | bytes 7454720 | tf_op jit(solution)/shard_map/dot_general | solution.py:14
  190.9 118.0 %all-reduce.9.cloned.1.call-done = bf16[128,384]{1,0:T(8,128)(2,1)} async-done(((bf16[128,384]{1,0:T(8,128)(2,1)}), bf16[128,384]{1,0:T(8,128)(2,1)}) %all-reduce.9.cloned.1.call-update) | async-done | bytes 98320 | tf_op jit(solution)/shard_map/psum | solution.py:144
  308.9 1.9 fusion.129
  (67 shorter events, 3.4 us)
Async XLA Ops:
  7.2 16.5 %copy-start = (bf16[2,4,40,5120]{3,2,1,0:T(8,128)(2,1)S(1)}, bf16[2,4,40,5120]{3,2,1,0:T(8,128)(2,1)}, u32[]{:S(2)}) copy-start(bf16[2,4,40,5120]{3,2,1,0:T(8,128)(2,1)} %param.19) | copy-start | bytes 9830404
  7.2 105.7 %all-reduce.5.cloned.1.call-start = ((), (), s32[]{:S(2)}) async-start(), calls=%async_computation.2 | async-start | bytes 589824 | tf_op jit(solution)/shard_map/psum | solution.py:97
  7.2 18.1 %collective-permute-start = (bf16[2,4,40,128]{3,2,1,0:T(8,128)(2,1)}, bf16[2,4,40,128]{3,2,1,0:T(8,128)(2,1)S(1)}, u32[]{:S(2)}, u32[]{:S(2)}) collective-permute-start(bf16[2,4,40,128]{3,2,1,0:T(8,128)(2,1)} %param.10), channel_id=1, source_target_pairs={{0,1},{1,2},{2,3},{3,4},{4,5},{5,6},{6,7},{7,8},{8,9},{9,10},{10,1... | collective-permute-start | bytes 245768 | tf_op jit(solution)/shard_map/ppermute | solution.py:86
  9.4 7.6 %copy-start.14 = (bf16[160,384]{1,0:T(8,128)(2,1)S(1)}, bf16[160,384]{1,0:T(8,128)(2,1)}, u32[]{:S(2)}) copy-start(bf16[160,384]{1,0:T(8,128)(2,1)} %param.16) | copy-start | bytes 368644
  15.4 2.8 copy-start.6
  20.1 117.9 %all-reduce.7.cloned.1.call-start = ((), (), s32[]{:S(2)}) async-start(), calls=%async_computation.3 | async-start | bytes 589824 | tf_op jit(solution)/shard_map/psum | solution.py:97
  20.1 3.6 %copy-start.5 = (bf16[128,5120]{1,0:T(8,128)(2,1)S(1)}, bf16[128,5120]{1,0:T(8,128)(2,1)}, u32[]{:S(2)}) copy-start(bf16[128,5120]{1,0:T(8,128)(2,1)} %param.18) | copy-start | bytes 3932164
  23.7 7.2 %copy-start.3 = (f32[256,256]{1,0:T(8,128)}, f32[256,256]{1,0:T(8,128)S(1)}, u32[]{:S(2)}) copy-start(f32[256,256]{1,0:T(8,128)S(1)} %fusion.148) | copy-start | bytes 786436
  23.7 1.7 copy-start.13
  25.4 1.2 copy-start.8
  138.0 2.5 copy-start.4
  139.1 1.3 copy-start.10
  139.1 2.5 copy-start.15
  139.4 0.8 copy-start.1
  139.4 3.2 %copy-start.12 = (bf16[320,128]{1,0:T(8,128)(2,1)S(1)}, bf16[320,128]{1,0:T(8,128)(2,1)}, u32[]{:S(2)}) copy-start(bf16[320,128]{1,0:T(8,128)(2,1)} %convolution_convert_fusion.4) | copy-start | bytes 245764
  141.9 0.7 copy-start.7
  143.7 10.8 %all-to-all-start = ((bf16[2,160,512]{2,0,1:T(2,128)(2,1)}), bf16[2,160,512]{2,0,1:T(2,128)(2,1)}, u32[]{:S(2)}, u32[]{:S(2)}) async-start(bf16[2,160,512]{2,0,1:T(2,128)(2,1)} %copy.12), calls=%async_computation | async-start | bytes 655360 | tf_op jit(solution)/shard_map/all_to_all | solution.py:119
  148.2 160.7 %all-reduce.9.cloned.1.call-start = ((), (), s32[]{:S(2)}) async-start(), calls=%async_computation.4 | async-start | bytes 196608 | tf_op jit(solution)/shard_map/psum | solution.py:144
  158.0 2.5 copy-start.9
  180.6 2.4 copy-start.2
  180.6 2.4 copy-start.11
  183.3 1.9 slice-start
Sparse Core Ops, SparseCore 0:
  20.2 92.6 all-reduce.4
  115.1 22.7 all-reduce.6
  185.3 123.5 all-reduce.8
